TPU v7x, 32 devices: a whole 2x2x4 slice. The times are simulated.
32 devices in a mesh: ctx: 8 (over z, x), tp: 4 (over y, core).
Axes of the slice: x: 2, y: 2, z: 4, core: 2. Of those that a mesh axis runs over, the one named last changes fastest.
Arguments:
- q_nope: bfloat16 [8, 128, 128], P('ctx', 'tp'), may hold values from -6 to 6
- q_rope: bfloat16 [8, 128, 64], P('ctx', 'tp'), may hold values from -256 to 256
- w_uk: bfloat16 [128, 128, 512], P('tp'), may hold values from -0.5 to 0.5
- w_uv: bfloat16 [128, 512, 128], P('tp'), may hold values from -3 to 3
- w_out: bfloat16 [16384, 7168], P('tp', 'ctx'), may hold values from -0.046875 to 0.046875
- prefix_cache: bfloat16 [32768, 576], P('ctx'), may hold values from -6 to 6
- block_table: int32 [512], P('ctx'), may hold values from 0 to 511, each once
- prefix_len: int32 [8], replicated, may hold values from 8192 to 32768
- suffix_cache: bfloat16 [8, 256, 576], P('ctx'), may hold values from -12 to 12
- suffix_len: int32 [8], P('ctx'), may hold values from 2 to 256
Outputs:
- layer_out: bfloat16 [8, 7168], P('tp', 'ctx')
Inputs may be any that keep to these rules, and one draw needn't show every extreme that they name: A permutation: slots b * 64 to b * 64 + 63 of prefix_cache hold prefix positions block_table[b] * 64 onwards.
All inputs are finite; a program needn't handle non-finite values.
Results may differ from a plain program's by a relative error of at most 0.0078.
Values may be sent and summed in bfloat16 or wider, within the bound.
A program may use at most 64 MiB of HBM per device.

v0:
```python
import jax
import jax.numpy as jnp
from jax import lax
from jax.sharding import PartitionSpec as P

LAT = 512
ROPE = 64
NOPE = 128
BLOCK = 64


masked_value = -1e30


def partial_stats(scores, visible, values, pattern):
    row_peak = jnp.max(jnp.where(visible, scores, masked_value), axis=2)
    weights = jnp.where(visible, jnp.exp(scores - row_peak[:, :, None]), 0.0).astype(jnp.bfloat16)
    row_mass = jnp.sum(weights, axis=2, dtype=jnp.float32)
    row_weighted = jnp.einsum(pattern, weights, values, preferred_element_type=jnp.float32)
    return (row_peak, row_mass, row_weighted)


def value_project(latent, value_weight):
    return jnp.einsum("rhc,hcv->rhv", latent, value_weight, precision=lax.Precision.HIGHEST)


def on_device(
    q_nope,
    q_rope,
    w_uk,
    w_uv,
    w_out,
    prefix_cache,
    block_table,
    prefix_len,
    suffix_cache,
    suffix_len,
):
    softmax_scale = (NOPE + ROPE) ** (-0.5)
    q_latent = jnp.einsum("rhn,hnc->rhc", q_nope, w_uk, preferred_element_type=jnp.float32).astype(
        jnp.bfloat16
    )
    own_queries = jnp.concatenate([q_latent, q_rope], axis=2)
    all_queries = lax.all_gather(own_queries, "ctx", axis=0, tiled=True)
    ctx_count = lax.axis_size("ctx")
    own_count = own_queries.shape[0]
    value_weight = w_uv.astype(jnp.float32)
    positions = (
        block_table[:, None] * BLOCK + jnp.arange(BLOCK, dtype=jnp.int32)[None, :]
    ).reshape(-1)
    visible = (positions[None, :] < prefix_len[:, None])[:, None, :]
    scores = (
        jnp.einsum("rhc,tc->rht", all_queries, prefix_cache, preferred_element_type=jnp.float32)
        * softmax_scale
    )
    row_peak, row_mass, row_weighted = partial_stats(
        scores, visible, prefix_cache[:, :LAT], "rht,tc->rhc"
    )
    suffix_scores = (
        jnp.einsum("rhc,rtc->rht", own_queries, suffix_cache, preferred_element_type=jnp.float32)
        * softmax_scale
    )
    suffix_slots = jnp.arange(suffix_cache.shape[1], dtype=jnp.int32)
    suffix_visible = (suffix_slots[None, :] < suffix_len[:, None])[:, None, :]
    tail_peak, tail_mass, tail_weighted = partial_stats(
        suffix_scores, suffix_visible, suffix_cache[:, :, :LAT], "rht,rtc->rhc"
    )

    def by_owner(values):
        return values.reshape((ctx_count, own_count) + values.shape[1:])

    got_peak, got_mass, got_weighted = (
        lax.all_to_all(by_owner(row_peak), "ctx", split_axis=0, concat_axis=0, tiled=True),
        lax.all_to_all(by_owner(row_mass), "ctx", split_axis=0, concat_axis=0, tiled=True),
        lax.all_to_all(by_owner(row_weighted), "ctx", split_axis=0, concat_axis=0, tiled=True),
    )
    highest = jnp.maximum(jnp.max(got_peak, axis=0), tail_peak)
    factors = jnp.exp(got_peak - highest[None])
    tail_factor = jnp.exp(tail_peak - highest)
    total_mass = jnp.sum(factors * got_mass, axis=0) + tail_factor * tail_mass
    total_weighted = (
        jnp.sum(factors[..., None] * got_weighted, axis=0) + tail_factor[:, :, None] * tail_weighted
    )
    head_values = value_project(total_weighted / total_mass[:, :, None], value_weight).astype(
        jnp.bfloat16
    )
    flat_values = head_values.reshape(own_count, -1)
    every_value = lax.all_gather(flat_values, "ctx", axis=0, tiled=True)
    return lax.psum_scatter(
        jnp.dot(every_value, w_out, preferred_element_type=jnp.float32),
        "tp",
        scatter_dimension=0,
        tiled=True,
    ).astype(jnp.bfloat16)


def solution(mesh):
    placed = (
        P("ctx", "tp", None),
        P("ctx", "tp", None),
        P("tp", None, None),
        P("tp", None, None),
        P("tp", "ctx"),
        P("ctx", None),
        P("ctx"),
        P(),
        P("ctx", None, None),
        P("ctx"),
    )
    return jax.shard_map(
        on_device, mesh=mesh, in_specs=placed, out_specs=P("tp", "ctx"), check_vma=False
    )
```

profile of v0, /device:TPU:0, one launch (start us, length us, event | category | flops | bytes accessed | tf_op | source)
XLA Modules:
  0.0 129.5 jit_solution(10840114998855403633)
XLA Ops:
  0.0 0.0 copy-start
  0.0 0.7 broadcast_multiply_fusion
  0.7 0.1 iota_add_fusion
  0.8 0.1 add.38
  0.9 0.0 copy-done
  0.9 3.0 %fusion.20 = bf16[32,1,512]{2,1,0:T(2,128)(2,1)S(1)} fusion(bf16[32,128,512]{2,1,0:T(8,128)(2,1)} %param.12, bf16[32,128,1]{1,0,2:T(8,128)(2,1)S(1)} %bitcast.55), kind=kOutput, calls=%fused_computation.32 | convolution fusion | flops 4194304 | bytes 4235264 | tf_op jit(solution)/shard_map/rhn,hnc->rhc/dot_general | solution.py:40
  3.9 0.0 copy-done.3
  3.9 32.7 %all_gather.6 = bf16[8,32,576]{2,1,0:T(8,128)(2,1)S(1)} all-gather(bf16[1,32,576]{2,1,0:T(8,128)(2,1)S(1)} %pad_maximum_fusion), channel_id=1, replica_groups=mesh['ctx'=8,'tp'=4] {'ctx'}, dimensions={0}, use_global_device_ids=true | all-gather | bytes 331776 | tf_op jit(solution)/shard_map/all_gather | solution.py:44
  36.6 0.0 copy-done.4
  36.6 0.1 broadcast_compare_fusion
  36.7 2.7 %select_reduce_fusion = (f32[8,32]{1,0:T(8,128)}, f32[8,32,4096]{2,1,0:T(8,128)S(1)}) fusion(pred[8,4096]{1,0:T(8,128)(4,1)S(1)} %broadcast_compare_fusion, bf16[8,32,576]{2,1,0:T(8,128)(2,1)S(1)} %all_gather.6, bf16[4096,576]{0,1:T(8,128)(2,1)S(1)} %copy-done.5), kind=kOutput, calls=%fused_computation.7 | convolution fusion | flops 1211105024 | bytes 9241600 | tf_op jit(solution)/shard_map/rhc,tc->rht/dot_general | solution.py:53
  39.4 1.9 %copy-done.1 = f32[8,32,4096]{2,1,0:T(8,128)} copy-done((f32[8,32,4096]{2,1,0:T(8,128)}, f32[8,32,4096]{2,1,0:T(8,128)S(1)}, u32[]{:S(2)}) %copy-start.1) | copy-done | bytes 4194328
  41.3 1.7 %convert_reduce_fusion = f32[8,32]{1,0:T(8,128)S(1)} fusion(f32[8,32,4096]{2,1,0:T(8,128)S(1)} %get-tuple-element.10, f32[8,32]{1,0:T(8,128)} %get-tuple-element.9, pred[8,4096]{1,0:T(8,128)(4,1)S(1)} %broadcast_compare_fusion), kind=kLoop, calls=%fused_computation.4 | loop fusion | flops 5242624 | bytes 4229120 | tf_op jit(solution)/shard_map/reduce_sum | solution.py:18
  43.0 11.8 %all_to_all.15 = f32[8,1,32]{2,1,0:T(1,128)S(1)} all-to-all(f32[8,1,32]{2,1,0:T(1,128)S(1)} %bitcast.60), channel_id=1, replica_groups=mesh['ctx'=8,'tp'=4] {'ctx'}, dimensions={0} | all-to-all | bytes 2048 | tf_op jit(solution)/shard_map/all_to_all | solution.py:74
  54.9 3.2 %all-to-all-start = ((f32[8,1,32]{2,1,0:T(1,128)}), f32[8,1,32]{2,1,0:T(1,128)S(1)}, u32[]{:S(2)}, u32[]{:S(2)}) async-start(f32[8,1,32]{2,1,0:T(1,128)} %bitcast.5), calls=%async_computation | async-start | bytes 8192 | tf_op jit(solution)/shard_map/all_to_all | solution.py:73
  58.1 0.0 copy-start.6
  58.1 0.0 copy-start.2
  58.1 5.6 %fusion.4 = f32[8,1,32,512]{3,2,1,0:T(8,128)} fusion(bf16[4096,576]{0,1:T(8,128)(2,1)} %param.15, f32[8,32,4096]{2,1,0:T(8,128)} %copy-done.1, f32[8,32]{1,0:T(8,128)} %get-tuple-element.9, pred[8,4096]{1,0:T(8,128)(4,1)S(1)} %broadcast_compare_fusion), kind=kOutput, calls=%fused_computation.8 | convolution fusion | flops 1076887552 | bytes 8949760 | tf_op jit(solution)/shard_map/rht,tc->rhc/dot_general | solution.py:19
  63.7 0.8 all-to-all-done
  64.5 5.1 %all-to-all-start.1 = ((f32[8,1,32,512]{3,2,1,0:T(8,128)}), f32[8,1,32,512]{3,2,1,0:T(8,128)S(1)}, u32[]{:S(2)}, u32[]{:S(2)}) async-start(f32[8,1,32,512]{3,2,1,0:T(8,128)} %fusion.4), calls=%async_computation.1 | async-start | bytes 1048576 | tf_op jit(solution)/shard_map/all_to_all | solution.py:75
  70.3 0.7 dynamic-slice
  71.7 0.0 copy-done.2
  71.7 0.3 select_reduce_fusion.1
  72.0 0.2 convert_reduce_fusion.1
  72.2 7.8 %all-to-all-done.1 = f32[8,1,32,512]{3,2,1,0:T(8,128)S(1)} async-done(((f32[8,1,32,512]{3,2,1,0:T(8,128)}), f32[8,1,32,512]{3,2,1,0:T(8,128)S(1)}, u32[]{:S(2)}, u32[]{:S(2)}) %all-to-all-start.1) | async-done | bytes 524320 | tf_op jit(solution)/shard_map/all_to_all | solution.py:75
  80.0 0.1 multiply_reduce_fusion
  80.1 0.2 fusion.9
  80.3 3.5 %fusion.16 = f32[32,1,128]{2,1,0:T(1,128)S(1)} fusion(bf16[32,512,128]{2,1,0:T(8,128)(2,1)} %param.13, f32[32,512,1]{1,0,2:T(8,128)S(1)} %fusion.9), kind=kOutput, calls=%fused_computation.22 | convolution fusion | flops 25165824 | bytes 4276224 | tf_op jit(solution)/shard_map/rhc,hcv->rhv/dot_general | solution.py:24
  83.9 30.5 %all-gather = bf16[8,1,4096]{2,1,0:T(2,128)(2,1)S(1)} all-gather(bf16[1,1,4096]{2,1,0:T(2,128)(2,1)S(1)} %reshape.166), channel_id=1, replica_groups=mesh['ctx'=8,'tp'=4] {'ctx'}, dimensions={0}, use_global_device_ids=true | all-gather | bytes 73728 | tf_op jit(solution)/shard_map/all_gather | solution.py:88
  114.4 4.1 %fusion.13 = f32[8,896]{1,0:T(8,128)S(1)} fusion(bf16[4096,896]{1,0:T(8,128)(2,1)} %param.14, bf16[8,1,4096]{2,1,0:T(2,128)(2,1)S(1)} %all-gather), kind=kOutput, calls=%fused_computation.18 | convolution fusion | flops 58720256 | bytes 7434240 | tf_op jit(solution)/shard_map/dot_general | solution.py:90
  118.6 10.3 %all-reduce = bf16[8,896]{1,0:T(8,128)(2,1)S(1)} all-reduce(f32[8,896]{1,0:T(8,128)S(1)} %fusion.13), channel_id=2, replica_groups=mesh['ctx'=8,'tp'=4] {'tp'}, use_global_device_ids=true, to_apply=%region_7.8.clone | all-reduce | flops 7168 | bytes 43008
  128.9 0.6 dynamic-slice_convert_fusion
  (15 shorter events, 0.1 us)
Async XLA Ops:
  0.0 0.9 copy-start
  0.0 3.9 %copy-start.3 = (bf16[1,32,64]{2,1,0:T(8,128)(2,1)S(1)}, bf16[1,32,64]{2,1,0:T(8,128)(2,1)}, u32[]{:S(2)}) copy-start(bf16[1,32,64]{2,1,0:T(8,128)(2,1)} %param.11) | copy-start | bytes 12292
  0.0 36.6 %copy-start.4 = (s32[8]{0:T(128)S(1)}, s32[8]{0:T(128)}, u32[]{:S(2)}) copy-start(s32[8]{0:T(128)} %param.17) | copy-start | bytes 100
  0.9 35.8 %copy-start.5 = (bf16[4096,576]{0,1:T(8,128)(2,1)S(1)}, bf16[4096,576]{0,1:T(8,128)(2,1)}, u32[]{:S(2)}) copy-start(bf16[4096,576]{0,1:T(8,128)(2,1)} %param.15) | copy-start | bytes 14155780
  39.4 1.9 %copy-start.1 = (f32[8,32,4096]{2,1,0:T(8,128)}, f32[8,32,4096]{2,1,0:T(8,128)S(1)}, u32[]{:S(2)}) copy-start(f32[8,32,4096]{2,1,0:T(8,128)S(1)} %get-tuple-element.10) | copy-start | bytes 12582916
  54.9 9.7 %all-to-all-start = ((f32[8,1,32]{2,1,0:T(1,128)}), f32[8,1,32]{2,1,0:T(1,128)S(1)}, u32[]{:S(2)}, u32[]{:S(2)}) async-start(f32[8,1,32]{2,1,0:T(1,128)} %bitcast.5), calls=%async_computation | async-start | bytes 8192 | tf_op jit(solution)/shard_map/all_to_all | solution.py:73
  58.1 12.2 %copy-start.6 = (u32[32]{0:T(128)S(1)}, u32[32]{0:T(128)}, u32[]{:S(2)}) copy-start(u32[32]{0:T(128)} %constant.17) | copy-start | bytes 388
  58.1 13.6 %copy-start.2 = (bf16[1,256,576]{1,2,0:T(8,128)(2,1)S(1)}, bf16[1,256,576]{1,2,0:T(8,128)(2,1)}, u32[]{:S(2)}) copy-start(bf16[1,256,576]{1,2,0:T(8,128)(2,1)} %param.18) | copy-start | bytes 884740
  64.5 15.5 %all-to-all-start.1 = ((f32[8,1,32,512]{3,2,1,0:T(8,128)}), f32[8,1,32,512]{3,2,1,0:T(8,128)S(1)}, u32[]{:S(2)}, u32[]{:S(2)}) async-start(f32[8,1,32,512]{3,2,1,0:T(8,128)} %fusion.4), calls=%async_computation.1 | async-start | bytes 1048576 | tf_op jit(solution)/shard_map/all_to_all | solution.py:75
where the time goes:
time: 130 us; the launch traced here: 129 us
  blocking collectives  85.4 us (66%)
  matrix products  19.4 us (15%)
  waiting for transfers between devices  8.58 us (7%)
  starting transfers between devices  8.34 us (6%)
  local copies, waits for them, and re-layouts  3.31 us (3%)
  other arithmetic  3 us (2%)
  between operations  1.49 us (1%)
    all_gather x1, blocking collectives, on_device(): all_queries = lax.all_gather(own_queries, 'ctx', axis=0, tiled=True)  32.7 us
    all_gather x1, blocking collectives, on_device(): every_value = lax.all_gather(flat_values, 'ctx', axis=0, tiled=True)  30.5 us
    all_to_all x1, blocking collectives, on_device(): lax.all_to_all(by_owner(row_mass), 'ctx', split_axis=0, concat_axis=0, ti...  11.8 us
    unnamed x1, blocking collectives  10.3 us
    all_to_all x1, waiting for transfers between devices, on_device(): lax.all_to_all(by_owner(row_weighted), 'ctx', split_axis=0, concat_axis=0...  7.78 us
    dot_general x2, matrix products, partial_stats(): jnp.einsum(pattern, weights, values, preferred_element_type=jnp.float32)  5.81 us
    all_to_all x1, starting transfers between devices, on_device(): lax.all_to_all(by_owner(row_weighted), 'ctx', split_axis=0, concat_axis=0...  5.12 us
    dot_general x1, matrix products, on_device(): jnp.dot(every_value, w_out, preferred_element_type=jnp.float32)  4.14 us
  transfers between devices with their start and end apart: 2, of which 2 were waited for; matrix products, arithmetic and copies ran while one was open for 5% of the time, Pallas kernels for 0%

commit v1 on v0

v1 whole, which is shorter than its diff:
```python
import functools

import jax
import jax.numpy as jnp
from jax import lax
from jax.experimental import pallas as pl
from jax.experimental.pallas import tpu as pltpu
from jax.sharding import PartitionSpec as P

LAT = 512
ROPE = 64
NOPE = 128
BLOCK = 64
LANES = 128
MASKED = -1e30
FLOOR = -1e29
LOG2E = 1.4426950408889634
MESH = pl.DeviceIdType.MESH


def thirds(x):
    a = x.astype(jnp.bfloat16).astype(jnp.float32)
    rest = x - a
    b = rest.astype(jnp.bfloat16).astype(jnp.float32)
    return a, b, (rest - b).astype(jnp.bfloat16).astype(jnp.float32)


def kernel(
    sizes,
    table_ref,
    prefix_len_ref,
    suffix_len_ref,
    q_nope_ref,
    q_rope_ref,
    w_uk_hbm,
    w_uv_hbm,
    w_out_hbm,
    prefix_hbm,
    suffix_hbm,
    out_ref,
    qn_all,
    qr_all,
    qn_rows,
    query,
    w_uk,
    w_uv,
    w_out,
    cache,
    mask,
    scores,
    peak,
    mass,
    weighted,
    msg,
    got,
    hv_all,
    part,
    part_got,
    load_sem,
    q_send,
    q_recv,
    m_send,
    m_recv,
    h_send,
    h_recv,
    p_send,
    p_recv,
):
    n, t, own, heads, requests, tokens, suffix, chunk = sizes
    rows = requests * heads
    block_rows = rows // n
    block_heads = max(1, block_rows // requests)
    head_rows = min(block_rows, requests)
    vdim = w_uv.shape[2]
    me = lax.axis_index("ctx")
    me_tp = lax.axis_index("tp")
    chunks = tokens // chunk

    loads = [pltpu.make_async_copy(w_uk_hbm, w_uk, load_sem.at[0])]
    for c in range(chunks):
        part_of = pl.ds(c * chunk, chunk)
        loads.append(
            pltpu.make_async_copy(prefix_hbm.at[part_of], cache.at[part_of], load_sem.at[1 + c])
        )
    for o in range(own):
        loads.append(
            pltpu.make_async_copy(
                suffix_hbm.at[o],
                cache.at[pl.ds(tokens + o * suffix, suffix)],
                load_sem.at[1 + chunks + o],
            )
        )
    first_head = (me * block_rows) // requests
    uv_load = pltpu.make_async_copy(
        w_uv_hbm.at[pl.ds(first_head, block_heads)], w_uv, load_sem.at[1 + chunks + own]
    )
    out_load = pltpu.make_async_copy(w_out_hbm, w_out, load_sem.at[2 + chunks + own])
    for load in loads:
        load.start()
    uv_load.start()
    out_load.start()

    barrier = pltpu.get_barrier_semaphore()
    for k in range(1, n):
        pl.semaphore_signal(
            barrier, inc=1, device_id=(lax.rem(me + k, n), me_tp), device_id_type=MESH
        )
    for k in range(1, t):
        pl.semaphore_signal(
            barrier, inc=1, device_id=(me, lax.rem(me_tp + k, t)), device_id_type=MESH
        )
    pl.semaphore_wait(barrier, n - 1 + t - 1)

    q_copies = []
    for k in range(1, n):
        to = (lax.rem(me + k, n), me_tp)
        for i, (src, dst) in enumerate(((q_nope_ref, qn_all), (q_rope_ref, qr_all))):
            copy = pltpu.make_async_remote_copy(
                src_ref=src,
                dst_ref=dst.at[pl.ds(me * own, own)],
                send_sem=q_send.at[i, k],
                recv_sem=q_recv.at[i, k],
                device_id=to,
                device_id_type=MESH,
            )
            copy.start()
            q_copies.append(copy)
    qn_all[pl.ds(me * own, own)] = q_nope_ref[...]
    qr_all[pl.ds(me * own, own)] = q_rope_ref[...]

    row = lax.broadcasted_iota(jnp.int32, (requests, LANES), 0)
    lane = lax.broadcasted_iota(jnp.int32, (requests, LANES), 1)
    limit = jnp.zeros((requests, LANES), jnp.int32)
    for r in range(requests):
        limit = jnp.where(row == r, prefix_len_ref[r], limit)
    per_tile = LANES // BLOCK
    for i in range(tokens // LANES):
        position = lane + table_ref[i * per_tile] * BLOCK
        for j in range(1, per_tile):
            moved = lane + (table_ref[i * per_tile + j] * BLOCK - j * BLOCK)
            position = jnp.where(lane >= j * BLOCK, moved, position)
        mask[:, i * LANES : (i + 1) * LANES] = jnp.where(position < limit, 0.0, MASKED)
    for o in range(own):
        for i in range(suffix // LANES):
            slot = lane + i * LANES
            start = tokens + o * suffix + i * LANES
            seen = (slot < suffix_len_ref[o]) & (row == me * own + o)
            mask[:, start : start + LANES] = jnp.where(seen, 0.0, MASKED)

    to_row = lax.broadcasted_iota(jnp.int32, (rows, rows), 0)
    from_row = lax.broadcasted_iota(jnp.int32, (rows, rows), 1)
    wanted = (to_row % requests) * heads + to_row // requests
    shuffle = jnp.where(from_row == wanted, 1.0, 0.0).astype(jnp.bfloat16)
    for copy in q_copies:
        copy.wait()
    qn_rows[...] = jnp.dot(
        shuffle, qn_all[...].reshape(rows, NOPE), preferred_element_type=jnp.float32
    )
    query[:, LAT:] = jnp.dot(
        shuffle, qr_all[...].reshape(rows, ROPE), preferred_element_type=jnp.float32
    ).astype(jnp.bfloat16)
    loads[0].wait()
    group = 8

    def absorb(g, carry):
        latents = []
        for j in range(group):
            h = g * group + j
            q = qn_rows[pl.ds(pl.multiple_of(h * requests, requests), requests), :]
            latents.append(
                jnp.dot(q.astype(jnp.bfloat16), w_uk[h], preferred_element_type=jnp.float32)
            )
        at = pl.multiple_of(g * (group * requests), group * requests)
        query[pl.ds(at, group * requests), :LAT] = jnp.concatenate(latents, axis=0).astype(
            jnp.bfloat16
        )
        return carry

    lax.fori_loop(0, heads // group, absorb, 0)

    scale = LOG2E * (NOPE + ROPE) ** (-0.5)
    spans = [(c * chunk, chunk) for c in range(chunks)]
    spans += [(tokens + o * suffix, suffix) for o in range(own)]
    for i, (start, length) in enumerate(spans):
        loads[1 + i].wait()
        s = lax.dot_general(
            query[...],
            cache[start : start + length, :],
            (((1,), (1,)), ((), ())),
            preferred_element_type=jnp.float32,
        )
        s = (s * scale).reshape(heads, requests, length) + mask[:, start : start + length][None]
        s = s.reshape(rows, length)
        scores[:, start : start + length] = s
        top = s[:, :LANES]
        for j in range(1, length // LANES):
            top = jnp.maximum(top, s[:, j * LANES : (j + 1) * LANES])
        peak[...] = top if i == 0 else jnp.maximum(peak[...], top)
    highest = jnp.maximum(jnp.max(peak[...], axis=1, keepdims=True), FLOOR)
    peak[...] = jnp.broadcast_to(highest, (rows, LANES))
    for i, (start, length) in enumerate(spans):
        p = jnp.exp2(scores[:, start : start + length] - peak[:, :1]).astype(jnp.bfloat16)
        wide = p.astype(jnp.float32)
        total = wide[:, :LANES]
        for j in range(1, length // LANES):
            total = total + wide[:, j * LANES : (j + 1) * LANES]
        mass[...] = total if i == 0 else mass[...] + total
        term = jnp.dot(
            p, cache[start : start + length, :LAT], preferred_element_type=jnp.float32
        )
        weighted[...] = term if i == 0 else weighted[...] + term

    sums = jnp.sum(mass[...], axis=1, keepdims=True)
    at_lane = lax.broadcasted_iota(jnp.int32, (rows, LANES), 1)
    stats = jnp.zeros((rows, LANES), jnp.float32)
    for i, piece in enumerate(thirds(peak[:, :1]) + thirds(sums)):
        stats = jnp.where(at_lane == i, piece, stats)
    msg[:, :, :LAT] = weighted[...].astype(jnp.bfloat16).reshape(n, block_rows, LAT)
    msg[:, :, LAT:] = stats.astype(jnp.bfloat16).reshape(n, block_rows, LANES)
    m_copies = []
    for k in range(1, n):
        to = lax.rem(me + k, n)
        copy = pltpu.make_async_remote_copy(
            src_ref=msg.at[to],
            dst_ref=got.at[k],
            send_sem=m_send.at[k],
            recv_sem=m_recv.at[k],
            device_id=(to, me_tp),
            device_id_type=MESH,
        )
        copy.start()
        m_copies.append(copy)
    got[0] = msg[me]
    uv_load.wait()
    for copy in m_copies:
        copy.wait()

    tops, totals = [], []
    for k in range(n):
        stat = got[k, :, LAT:].astype(jnp.float32)
        tops.append(stat[:, 0:1] + stat[:, 1:2] + stat[:, 2:3])
        totals.append(stat[:, 3:4] + stat[:, 4:5] + stat[:, 5:6])
    best = functools.reduce(jnp.maximum, tops)
    factors = [jnp.exp2(top - best) for top in tops]
    whole = sum(f * m for f, m in zip(factors, totals))
    latent = sum(f * got[k, :, :LAT].astype(jnp.float32) for k, f in enumerate(factors)) / whole
    values = []
    for j in range(block_heads):
        pieces = jnp.concatenate(thirds(latent[j * head_rows : (j + 1) * head_rows]), axis=0)
        y = jnp.dot(pieces.astype(jnp.bfloat16), w_uv[j], preferred_element_type=jnp.float32)
        values.append(y[:head_rows] + y[head_rows : 2 * head_rows] + y[2 * head_rows :])
    hv_all[me] = jnp.concatenate(values, axis=1).astype(jnp.bfloat16)
    h_copies = []
    for k in range(1, n):
        copy = pltpu.make_async_remote_copy(
            src_ref=hv_all.at[me],
            dst_ref=hv_all.at[me],
            send_sem=h_send.at[k],
            recv_sem=h_recv.at[k],
            device_id=(lax.rem(me + k, n), me_tp),
            device_id_type=MESH,
        )
        copy.start()
        h_copies.append(copy)
    out_load.wait()

    if block_rows >= requests:
        depth = block_heads * vdim
        total = None
        for k in range(n):
            source = lax.rem(me + n - k, n)
            if k:
                h_copies[k - 1].wait_recv()
            term = jnp.dot(
                hv_all[source],
                w_out[pl.ds(pl.multiple_of(source * depth, depth), depth), :],
                preferred_element_type=jnp.float32,
            )
            total = term if k == 0 else total + term
    else:
        for copy in h_copies:
            copy.wait_recv()
        split = requests // block_rows
        total = None
        for h in range(heads):
            lhs = jnp.concatenate([hv_all[h * split + i] for i in range(split)], axis=0)
            term = jnp.dot(
                lhs, w_out[h * vdim : (h + 1) * vdim, :], preferred_element_type=jnp.float32
            )
            total = term if h == 0 else total + term
    for copy in h_copies:
        copy.wait_send()

    share = requests // t
    for i in range(t):
        part[i] = total[i * share : (i + 1) * share]
    p_copies = []
    for k in range(1, t):
        to = lax.rem(me_tp + k, t)
        copy = pltpu.make_async_remote_copy(
            src_ref=part.at[to],
            dst_ref=part_got.at[k],
            send_sem=p_send.at[k],
            recv_sem=p_recv.at[k],
            device_id=(me, to),
            device_id_type=MESH,
        )
        copy.start()
        p_copies.append(copy)
    result = part[me_tp]
    for k in range(1, t):
        p_copies[k - 1].wait()
        result = result + part_got[k]
    out_ref[...] = result.astype(jnp.bfloat16)


def on_device(
    n,
    t,
    q_nope,
    q_rope,
    w_uk,
    w_uv,
    w_out,
    prefix_cache,
    block_table,
    prefix_len,
    suffix_cache,
    suffix_len,
):
    own, heads, _ = q_nope.shape
    requests = own * n
    tokens, width = prefix_cache.shape
    suffix = suffix_cache.shape[1]
    chunk = 1024 if tokens % 1024 == 0 else tokens
    chunks = tokens // chunk
    slots = tokens + own * suffix
    rows = requests * heads
    block_rows = rows // n
    block_heads = max(1, block_rows // requests)
    head_rows = min(block_rows, requests)
    vdim = w_uv.shape[2]
    columns = w_out.shape[1]
    share = requests // t
    bf, f32 = jnp.bfloat16, jnp.float32
    sizes = (n, t, own, heads, requests, tokens, suffix, chunk)
    smem = pl.BlockSpec(memory_space=pltpu.SMEM)
    vmem = pl.BlockSpec(memory_space=pltpu.VMEM)
    hbm = pl.BlockSpec(memory_space=pl.ANY)
    dma = pltpu.SemaphoreType.DMA
    return pl.pallas_call(
        functools.partial(kernel, sizes),
        out_shape=jax.ShapeDtypeStruct((share, columns), bf),
        in_specs=[smem] * 3 + [vmem] * 2 + [hbm] * 5,
        out_specs=vmem,
        scratch_shapes=[
            pltpu.VMEM((requests, heads, NOPE), bf),
            pltpu.VMEM((requests, heads, ROPE), bf),
            pltpu.VMEM((rows, NOPE), f32),
            pltpu.VMEM((rows, width), bf),
            pltpu.VMEM(w_uk.shape, bf),
            pltpu.VMEM((block_heads,) + w_uv.shape[1:], bf),
            pltpu.VMEM(w_out.shape, bf),
            pltpu.VMEM((slots, width), bf),
            pltpu.VMEM((requests, slots), f32),
            pltpu.VMEM((rows, slots), f32),
            pltpu.VMEM((rows, LANES), f32),
            pltpu.VMEM((rows, LANES), f32),
            pltpu.VMEM((rows, LAT), f32),
            pltpu.VMEM((n, block_rows, LAT + LANES), bf),
            pltpu.VMEM((n, block_rows, LAT + LANES), bf),
            pltpu.VMEM((n, head_rows, block_heads * vdim), bf),
            pltpu.VMEM((t, share, columns), f32),
            pltpu.VMEM((t, share, columns), f32),
            dma((3 + chunks + own,)),
            dma((2, n)),
            dma((2, n)),
            dma((n,)),
            dma((n,)),
            dma((n,)),
            dma((n,)),
            dma((t,)),
            dma((t,)),
        ],
        compiler_params=pltpu.CompilerParams(
            collective_id=0, has_side_effects=True, vmem_limit_bytes=60 * 1024 * 1024
        ),
    )(
        block_table,
        prefix_len,
        suffix_len,
        q_nope,
        q_rope,
        w_uk,
        w_uv,
        w_out,
        prefix_cache,
        suffix_cache,
    )


def solution(mesh):
    placed = (
        P("ctx", "tp", None),
        P("ctx", "tp", None),
        P("tp", None, None),
        P("tp", None, None),
        P("tp", "ctx"),
        P("ctx", None),
        P("ctx"),
        P(),
        P("ctx", None, None),
        P("ctx"),
    )
    return jax.shard_map(
        functools.partial(on_device, mesh.shape["ctx"], mesh.shape["tp"]),
        mesh=mesh,
        in_specs=placed,
        out_specs=P("tp", "ctx"),
        check_vma=False,
    )
```

time: 130 us -> 48.7 us (0.37)
  blocking collectives: 85.4 us -> 0 us
  Pallas kernels: 0 us -> 36.9 us
  matrix products: 19.4 us -> 0 us
  waiting for transfers between devices: 8.58 us -> 0 us
  starting transfers between devices: 8.34 us -> 0 us
  local copies, waits for them, and re-layouts: 3.31 us -> 10.8 us
  other arithmetic: 3 us -> 0 us
    all_gather x2 -> x0, blocking collectives: 63.2 us -> none  [the longest x1 32.7 us: on_device(): all_queries = lax.all_gather(own_queries, 'ctx', axis=0, tiled=True)]
    pallas_call x0 -> x1, Pallas kernels: none -> 36.9 us  [on_device(): pl.pallas_call(functools.partial(kernel, sizes), out_shape=jax.ShapeDtype...]
    dot_general x7 -> x0, matrix products: 19.4 us -> none  [the longest x2 5.81 us: partial_stats(): jnp.einsum(pattern, weights, values, preferred_element_type=jnp.float32)]
    all_to_all x1 -> x0, blocking collectives: 11.8 us -> none  [on_device(): lax.all_to_all(by_owner(row_mass), 'ctx', split_axis=0, concat_axis=0, ti...]
    unnamed x1 -> x0, blocking collectives: 10.3 us -> none
    all_to_all x2 -> x0, waiting for transfers between devices: 8.58 us -> none  [the longest x1 7.78 us: on_device(): lax.all_to_all(by_owner(row_weighted), 'ctx', split_axis=0, concat_axis=0...]
    all_to_all x2 -> x0, starting transfers between devices: 8.34 us -> none  [the longest x1 5.12 us: on_device(): lax.all_to_all(by_owner(row_weighted), 'ctx', split_axis=0, concat_axis=0...]
    unnamed x16 -> x3, local copies, waits for them, and re-layouts: 2.63 us -> 10.8 us
  transfers between devices with their start and end apart: 2 -> 0, of which waited for: 2 -> 0; matrix products, arithmetic and copies ran while one was open for 5% -> 0% of each run, Pallas kernels for 0% -> 0%
where the time goes in v1:
time: 48.7 us; the launch traced here: 48.3 us
  Pallas kernels  36.9 us (76%)
  local copies, waits for them, and re-layouts  10.8 us (22%)
  between operations  0.66 us (1%)
    pallas_call x1, Pallas kernels, on_device(): pl.pallas_call(functools.partial(kernel, sizes), out_shape=jax.ShapeDtype...  36.9 us
    unnamed x3, local copies, waits for them, and re-layouts  10.8 us

profile of v1, /device:TPU:0, one launch (start us, length us, event | category | flops | bytes accessed | tf_op | source)
XLA Modules:
  0.0 48.3 jit_solution(5316012321833314198)
XLA Ops:
  0.7 1.9 %copy.12.suffix_hbm = bf16[1,256,576]{2,1,0:T(8,128)(2,1)} copy(bf16[1,256,576]{1,2,0:T(8,128)(2,1)} %param.18) | data formatting | bytes 589824 | tf_op args[8]
  2.5 7.6 %copy.11.prefix_hbm = bf16[4096,576]{1,0:T(8,128)(2,1)} copy(bf16[4096,576]{0,1:T(8,128)(2,1)} %param.15) | data formatting | bytes 9437184 | tf_op args[5]
  10.2 36.9 %shard_map.100 = bf16[2,896]{1,0:T(2,128)(2,1)} custom-call(s32[64]{0:T(128)} %table_ref.1, s32[8]{0:T(128)} %prefix_len_ref.1, s32[1]{0:T(128)S(6)} %copy.14.suffix_len_ref, bf16[1,32,128]{2,1,0:T(8,128)(2,1)} %q_nope_ref.1, bf16[1,32,64]{2,1,0:T(8,128)(2,1)} %q_rope_ref.1, bf16[32,128,512]{2,1,0:T(8,128)(2,1)} %w_uk_hbm.1, bf16[32,512,128]{2,1,0:T(8,128)(2,1)} %w_uv_hbm.1, ...), custom_call_target="tpu_custom_call" | custom-call | tf_op jit(solution)/shard_map/pallas_call | solution.py:351
  47.0 1.3 %copy.15 = bf16[2,896]{1,0:T(2,128)(2,1)} copy(bf16[2,896]{1,0:T(2,128)(2,1)} %shard_map.100) | data formatting | bytes 7168

commit v2 on v1

--- a/solution.py
+++ b/solution.py
@@ -80,13 +80,15 @@
     for c in range(chunks):
         part_of = pl.ds(c * chunk, chunk)
         loads.append(
-            pltpu.make_async_copy(prefix_hbm.at[part_of], cache.at[part_of], load_sem.at[1 + c])
+            pltpu.make_async_copy(
+                prefix_hbm.at[:, part_of], cache.at[:, part_of], load_sem.at[1 + c]
+            )
         )
     for o in range(own):
         loads.append(
             pltpu.make_async_copy(
                 suffix_hbm.at[o],
-                cache.at[pl.ds(tokens + o * suffix, suffix)],
+                cache.at[:, pl.ds(tokens + o * suffix, suffix)],
                 load_sem.at[1 + chunks + o],
             )
         )
@@ -181,56 +183,68 @@
     scale = LOG2E * (NOPE + ROPE) ** (-0.5)
     spans = [(c * chunk, chunk) for c in range(chunks)]
     spans += [(tokens + o * suffix, suffix) for o in range(own)]
-    for i, (start, length) in enumerate(spans):
-        loads[1 + i].wait()
-        s = lax.dot_general(
-            query[...],
-            cache[start : start + length, :],
-            (((1,), (1,)), ((), ())),
-            preferred_element_type=jnp.float32,
-        )
-        s = (s * scale).reshape(heads, requests, length) + mask[:, start : start + length][None]
-        s = s.reshape(rows, length)
-        scores[:, start : start + length] = s
-        top = s[:, :LANES]
-        for j in range(1, length // LANES):
-            top = jnp.maximum(top, s[:, j * LANES : (j + 1) * LANES])
-        peak[...] = top if i == 0 else jnp.maximum(peak[...], top)
-    highest = jnp.maximum(jnp.max(peak[...], axis=1, keepdims=True), FLOOR)
-    peak[...] = jnp.broadcast_to(highest, (rows, LANES))
-    for i, (start, length) in enumerate(spans):
-        p = jnp.exp2(scores[:, start : start + length] - peak[:, :1]).astype(jnp.bfloat16)
-        wide = p.astype(jnp.float32)
-        total = wide[:, :LANES]
-        for j in range(1, length // LANES):
-            total = total + wide[:, j * LANES : (j + 1) * LANES]
-        mass[...] = total if i == 0 else mass[...] + total
-        term = jnp.dot(
-            p, cache[start : start + length, :LAT], preferred_element_type=jnp.float32
-        )
-        weighted[...] = term if i == 0 else weighted[...] + term
-
-    sums = jnp.sum(mass[...], axis=1, keepdims=True)
-    at_lane = lax.broadcasted_iota(jnp.int32, (rows, LANES), 1)
-    stats = jnp.zeros((rows, LANES), jnp.float32)
-    for i, piece in enumerate(thirds(peak[:, :1]) + thirds(sums)):
-        stats = jnp.where(at_lane == i, piece, stats)
-    msg[:, :, :LAT] = weighted[...].astype(jnp.bfloat16).reshape(n, block_rows, LAT)
-    msg[:, :, LAT:] = stats.astype(jnp.bfloat16).reshape(n, block_rows, LANES)
+    half = n // 2
+    side = me // half
+    place = lax.rem(me, half)
+    part_rows = rows // 2
     m_copies = []
-    for k in range(1, n):
-        to = lax.rem(me + k, n)
-        copy = pltpu.make_async_remote_copy(
-            src_ref=msg.at[to],
-            dst_ref=got.at[k],
-            send_sem=m_send.at[k],
-            recv_sem=m_recv.at[k],
-            device_id=(to, me_tp),
-            device_id_type=MESH,
-        )
-        copy.start()
-        m_copies.append(copy)
-    got[0] = msg[me]
+    for turn in range(2):
+        part_side = lax.rem(side + 1 + turn, 2)
+        base = pl.multiple_of(part_side * part_rows, part_rows)
+        for i, (start, length) in enumerate(spans):
+            if turn == 0:
+                loads[1 + i].wait()
+            s = jnp.dot(
+                query[pl.ds(base, part_rows), :],
+                cache[:, start : start + length],
+                preferred_element_type=jnp.float32,
+            )
+            s = (s * scale).reshape(part_rows // requests, requests, length)
+            s = (s + mask[:, start : start + length][None]).reshape(part_rows, length)
+            scores[:, start : start + length] = s
+            top = s[:, :LANES]
+            for j in range(1, length // LANES):
+                top = jnp.maximum(top, s[:, j * LANES : (j + 1) * LANES])
+            peak[...] = top if i == 0 else jnp.maximum(peak[...], top)
+        highest = jnp.maximum(jnp.max(peak[...], axis=1, keepdims=True), FLOOR)
+        peak[...] = jnp.broadcast_to(highest, (part_rows, LANES))
+        for i, (start, length) in enumerate(spans):
+            p = jnp.exp2(scores[:, start : start + length] - peak[:, :1]).astype(jnp.bfloat16)
+            wide = p.astype(jnp.float32)
+            total = wide[:, :LANES]
+            for j in range(1, length // LANES):
+                total = total + wide[:, j * LANES : (j + 1) * LANES]
+            mass[...] = total if i == 0 else mass[...] + total
+            term = lax.dot_general(
+                p,
+                cache[:LAT, start : start + length],
+                (((1,), (1,)), ((), ())),
+                preferred_element_type=jnp.float32,
+            )
+            weighted[...] = term if i == 0 else weighted[...] + term
+
+        sums = jnp.sum(mass[...], axis=1, keepdims=True)
+        at_lane = lax.broadcasted_iota(jnp.int32, (part_rows, LANES), 1)
+        stats = jnp.zeros((part_rows, LANES), jnp.float32)
+        for i, piece in enumerate(thirds(peak[:, :1]) + thirds(sums)):
+            stats = jnp.where(at_lane == i, piece, stats)
+        slots = pl.ds(part_side * half, half)
+        msg[slots, :, :LAT] = weighted[...].astype(jnp.bfloat16).reshape(half, block_rows, LAT)
+        msg[slots, :, LAT:] = stats.astype(jnp.bfloat16).reshape(half, block_rows, LANES)
+        for k in range(turn, half):
+            to = part_side * half + lax.rem(place + k, half)
+            slot = turn * half + k
+            copy = pltpu.make_async_remote_copy(
+                src_ref=msg.at[to],
+                dst_ref=got.at[slot],
+                send_sem=m_send.at[slot],
+                recv_sem=m_recv.at[slot],
+                device_id=(to, me_tp),
+                device_id_type=MESH,
+            )
+            copy.start()
+            m_copies.append(copy)
+    got[half] = msg[me]
     uv_load.wait()
     for copy in m_copies:
         copy.wait()
@@ -361,12 +375,12 @@
             pltpu.VMEM(w_uk.shape, bf),
             pltpu.VMEM((block_heads,) + w_uv.shape[1:], bf),
             pltpu.VMEM(w_out.shape, bf),
-            pltpu.VMEM((slots, width), bf),
+            pltpu.VMEM((width, slots), bf),
             pltpu.VMEM((requests, slots), f32),
-            pltpu.VMEM((rows, slots), f32),
-            pltpu.VMEM((rows, LANES), f32),
-            pltpu.VMEM((rows, LANES), f32),
-            pltpu.VMEM((rows, LAT), f32),
+            pltpu.VMEM((rows // 2, slots), f32),
+            pltpu.VMEM((rows // 2, LANES), f32),
+            pltpu.VMEM((rows // 2, LANES), f32),
+            pltpu.VMEM((rows // 2, LAT), f32),
             pltpu.VMEM((n, block_rows, LAT + LANES), bf),
             pltpu.VMEM((n, block_rows, LAT + LANES), bf),
             pltpu.VMEM((n, head_rows, block_heads * vdim), bf),
@@ -394,8 +408,8 @@
         w_uk,
         w_uv,
         w_out,
-        prefix_cache,
-        suffix_cache,
+        prefix_cache.T,
+        jnp.swapaxes(suffix_cache, 1, 2),
     )
 
 

time: 48.7 us -> 36.7 us (0.75)
  local copies, waits for them, and re-layouts: 10.8 us -> 1.27 us
  Pallas kernels: 36.9 us -> 34.5 us
    unnamed x3 -> x1, local copies, waits for them, and re-layouts: 10.8 us -> 1.27 us
    pallas_call x1, Pallas kernels: 36.9 us -> 34.5 us  [on_device(): pl.pallas_call(functools.partial(kernel, sizes), out_shape=jax.ShapeDtype...]
where the time goes in v2:
time: 36.7 us; the launch traced here: 36.5 us
  Pallas kernels  34.5 us (94%)
  local copies, waits for them, and re-layouts  1.27 us (3%)
  between operations  0.66 us (2%)
    pallas_call x1, Pallas kernels, on_device(): pl.pallas_call(functools.partial(kernel, sizes), out_shape=jax.ShapeDtype...  34.5 us
    unnamed x1, local copies, waits for them, and re-layouts  1.27 us

profile of v2, /device:TPU:0, one launch (start us, length us, event | category | flops | bytes accessed | tf_op | source)
XLA Modules:
  0.0 36.5 jit_solution(13012557577032460969)
XLA Ops:
  0.7 34.5 %shard_map.100 = bf16[2,896]{1,0:T(2,128)(2,1)} custom-call(s32[64]{0:T(128)} %table_ref.1, s32[8]{0:T(128)} %prefix_len_ref.1, s32[1]{0:T(128)S(6)} %copy.12.suffix_len_ref, bf16[1,32,128]{2,1,0:T(8,128)(2,1)} %q_nope_ref.1, bf16[1,32,64]{2,1,0:T(8,128)(2,1)} %q_rope_ref.1, bf16[32,128,512]{2,1,0:T(8,128)(2,1)} %w_uk_hbm.1, bf16[32,512,128]{2,1,0:T(8,128)(2,1)} %w_uv_hbm.1, ...), custom_call_target="tpu_custom_call" | custom-call | tf_op jit(solution)/shard_map/pallas_call | solution.py:365
  35.2 1.3 %copy.13 = bf16[2,896]{1,0:T(2,128)(2,1)} copy(bf16[2,896]{1,0:T(2,128)(2,1)} %shard_map.100) | data formatting | bytes 7168

commit v3 on v2

--- a/solution.py
+++ b/solution.py
@@ -27,9 +27,9 @@
 
 def kernel(
     sizes,
-    table_ref,
-    prefix_len_ref,
     suffix_len_ref,
+    table_hbm,
+    prefix_len_hbm,
     q_nope_ref,
     q_rope_ref,
     w_uk_hbm,
@@ -56,7 +56,10 @@
     hv_all,
     part,
     part_got,
+    table_ref,
+    prefix_len_ref,
     load_sem,
+    small_sem,
     q_send,
     q_recv,
     m_send,
@@ -76,6 +79,20 @@
     me_tp = lax.axis_index("tp")
     chunks = tokens // chunk
 
+    mine = pl.ds(me * own, own)
+    smalls = [
+        pltpu.make_async_copy(src, dst, small_sem.at[i])
+        for i, (src, dst) in enumerate(
+            (
+                (table_hbm, table_ref),
+                (prefix_len_hbm, prefix_len_ref),
+                (q_nope_ref, qn_all.at[mine]),
+                (q_rope_ref, qr_all.at[mine]),
+            )
+        )
+    ]
+    for small in smalls:
+        small.start()
     loads = [pltpu.make_async_copy(w_uk_hbm, w_uk, load_sem.at[0])]
     for c in range(chunks):
         part_of = pl.ds(c * chunk, chunk)
@@ -97,11 +114,6 @@
         w_uv_hbm.at[pl.ds(first_head, block_heads)], w_uv, load_sem.at[1 + chunks + own]
     )
     out_load = pltpu.make_async_copy(w_out_hbm, w_out, load_sem.at[2 + chunks + own])
-    for load in loads:
-        load.start()
-    uv_load.start()
-    out_load.start()
-
     barrier = pltpu.get_barrier_semaphore()
     for k in range(1, n):
         pl.semaphore_signal(
@@ -111,6 +123,7 @@
         pl.semaphore_signal(
             barrier, inc=1, device_id=(me, lax.rem(me_tp + k, t)), device_id_type=MESH
         )
+    loads[0].start()
     pl.semaphore_wait(barrier, n - 1 + t - 1)
 
     q_copies = []
@@ -119,7 +132,7 @@
         for i, (src, dst) in enumerate(((q_nope_ref, qn_all), (q_rope_ref, qr_all))):
             copy = pltpu.make_async_remote_copy(
                 src_ref=src,
-                dst_ref=dst.at[pl.ds(me * own, own)],
+                dst_ref=dst.at[mine],
                 send_sem=q_send.at[i, k],
                 recv_sem=q_recv.at[i, k],
                 device_id=to,
@@ -127,8 +140,12 @@
             )
             copy.start()
             q_copies.append(copy)
-    qn_all[pl.ds(me * own, own)] = q_nope_ref[...]
-    qr_all[pl.ds(me * own, own)] = q_rope_ref[...]
+    for load in loads[1:]:
+        load.start()
+    uv_load.start()
+    out_load.start()
+    for small in smalls:
+        small.wait()
 
     row = lax.broadcasted_iota(jnp.int32, (requests, LANES), 0)
     lane = lax.broadcasted_iota(jnp.int32, (requests, LANES), 1)
@@ -265,32 +282,35 @@
         values.append(y[:head_rows] + y[head_rows : 2 * head_rows] + y[2 * head_rows :])
     hv_all[me] = jnp.concatenate(values, axis=1).astype(jnp.bfloat16)
     h_copies = []
-    for k in range(1, n):
-        copy = pltpu.make_async_remote_copy(
-            src_ref=hv_all.at[me],
-            dst_ref=hv_all.at[me],
-            send_sem=h_send.at[k],
-            recv_sem=h_recv.at[k],
-            device_id=(lax.rem(me + k, n), me_tp),
-            device_id_type=MESH,
-        )
-        copy.start()
-        h_copies.append(copy)
+    sources = []
+    for turn in range(2):
+        to_side = lax.rem(side + 1 + turn, 2)
+        for k in range(turn, half):
+            copy = pltpu.make_async_remote_copy(
+                src_ref=hv_all.at[me],
+                dst_ref=hv_all.at[me],
+                send_sem=h_send.at[turn * half + k],
+                recv_sem=h_recv.at[turn * half + k],
+                device_id=(to_side * half + lax.rem(place + k, half), me_tp),
+                device_id_type=MESH,
+            )
+            copy.start()
+            h_copies.append(copy)
+            sources.append(to_side * half + lax.rem(place + half - k, half))
     out_load.wait()
 
     if block_rows >= requests:
         depth = block_heads * vdim
         total = None
-        for k in range(n):
-            source = lax.rem(me + n - k, n)
-            if k:
-                h_copies[k - 1].wait_recv()
+        for source, copy in [(me, None)] + list(zip(sources, h_copies))[::-1]:
+            if copy is not None:
+                copy.wait_recv()
             term = jnp.dot(
                 hv_all[source],
                 w_out[pl.ds(pl.multiple_of(source * depth, depth), depth), :],
                 preferred_element_type=jnp.float32,
             )
-            total = term if k == 0 else total + term
+            total = term if copy is None else total + term
     else:
         for copy in h_copies:
             copy.wait_recv()
@@ -346,7 +366,7 @@
     requests = own * n
     tokens, width = prefix_cache.shape
     suffix = suffix_cache.shape[1]
-    chunk = 1024 if tokens % 1024 == 0 else tokens
+    chunk = 2048 if tokens % 2048 == 0 else tokens
     chunks = tokens // chunk
     slots = tokens + own * suffix
     rows = requests * heads
@@ -358,14 +378,13 @@
     share = requests // t
     bf, f32 = jnp.bfloat16, jnp.float32
     sizes = (n, t, own, heads, requests, tokens, suffix, chunk)
-    smem = pl.BlockSpec(memory_space=pltpu.SMEM)
     vmem = pl.BlockSpec(memory_space=pltpu.VMEM)
     hbm = pl.BlockSpec(memory_space=pl.ANY)
     dma = pltpu.SemaphoreType.DMA
     return pl.pallas_call(
         functools.partial(kernel, sizes),
         out_shape=jax.ShapeDtypeStruct((share, columns), bf),
-        in_specs=[smem] * 3 + [vmem] * 2 + [hbm] * 5,
+        in_specs=[pl.BlockSpec(memory_space=pltpu.SMEM)] + [hbm] * 9,
         out_specs=vmem,
         scratch_shapes=[
             pltpu.VMEM((requests, heads, NOPE), bf),
@@ -386,7 +405,10 @@
             pltpu.VMEM((n, head_rows, block_heads * vdim), bf),
             pltpu.VMEM((t, share, columns), f32),
             pltpu.VMEM((t, share, columns), f32),
+            pltpu.SMEM(block_table.shape, jnp.int32),
+            pltpu.SMEM(prefix_len.shape, jnp.int32),
             dma((3 + chunks + own,)),
+            dma((4,)),
             dma((2, n)),
             dma((2, n)),
             dma((n,)),
@@ -400,9 +422,9 @@
             collective_id=0, has_side_effects=True, vmem_limit_bytes=60 * 1024 * 1024
         ),
     )(
+        suffix_len,
         block_table,
         prefix_len,
-        suffix_len,
         q_nope,
         q_rope,
         w_uk,

time: 36.7 us -> 35.3 us (0.962)
  Pallas kernels: 34.5 us -> 33.2 us
    pallas_call x1, Pallas kernels: 34.5 us -> 33.2 us  [on_device(): pl.pallas_call(functools.partial(kernel, sizes), out_shape=jax.ShapeDtype...]
where the time goes in v3:
time: 35.3 us; the launch traced here: 35.1 us
  Pallas kernels  33.2 us (94%)
  local copies, waits for them, and re-layouts  1.27 us (4%)
  between operations  0.66 us (2%)
    pallas_call x1, Pallas kernels, on_device(): pl.pallas_call(functools.partial(kernel, sizes), out_shape=jax.ShapeDtype...  33.2 us
    unnamed x1, local copies, waits for them, and re-layouts  1.27 us

profile of v3, /device:TPU:0, one launch (start us, length us, event | category | flops | bytes accessed | tf_op | source)
XLA Modules:
  0.0 35.1 jit_solution(7709191109985270904)
XLA Ops:
  0.7 33.2 %shard_map.100 = bf16[2,896]{1,0:T(2,128)(2,1)} custom-call(s32[1]{0:T(128)S(6)} %copy.12.suffix_len_ref, s32[64]{0:T(128)} %table_hbm.1, s32[8]{0:T(128)} %prefix_len_hbm.1, bf16[1,32,128]{2,1,0:T(8,128)(2,1)} %q_nope_ref.1, bf16[1,32,64]{2,1,0:T(8,128)(2,1)} %q_rope_ref.1, bf16[32,128,512]{2,1,0:T(8,128)(2,1)} %w_uk_hbm.1, bf16[32,512,128]{2,1,0:T(8,128)(2,1)} %w_uv_hbm.1, ...), custom_call_target="tpu_custom_call" | custom-call | tf_op jit(solution)/shard_map/pallas_call | solution.py:384
  33.9 1.3 %copy.13 = bf16[2,896]{1,0:T(2,128)(2,1)} copy(bf16[2,896]{1,0:T(2,128)(2,1)} %shard_map.100) | data formatting | bytes 7168

commit v4 on v3

--- a/solution.py
+++ b/solution.py
@@ -53,6 +53,10 @@
     weighted,
     msg,
     got,
+    stat_msg,
+    stat_got,
+    stat_rows,
+    stat_columns,
     hv_all,
     part,
     part_got,
@@ -64,6 +68,8 @@
     q_recv,
     m_send,
     m_recv,
+    s_send,
+    s_recv,
     h_send,
     h_recv,
     p_send,
@@ -146,6 +152,8 @@
     out_load.start()
     for small in smalls:
         small.wait()
+
+    stat_rows[...] = jnp.zeros_like(stat_rows)
 
     row = lax.broadcasted_iota(jnp.int32, (requests, LANES), 0)
     lane = lax.broadcasted_iota(jnp.int32, (requests, LANES), 1)
@@ -242,12 +250,10 @@
 
         sums = jnp.sum(mass[...], axis=1, keepdims=True)
         at_lane = lax.broadcasted_iota(jnp.int32, (part_rows, LANES), 1)
-        stats = jnp.zeros((part_rows, LANES), jnp.float32)
-        for i, piece in enumerate(thirds(peak[:, :1]) + thirds(sums)):
-            stats = jnp.where(at_lane == i, piece, stats)
+        stats = jnp.where(at_lane == 0, peak[...], sums)
+        stat_msg[turn] = jnp.transpose(stats)[:2]
         slots = pl.ds(part_side * half, half)
-        msg[slots, :, :LAT] = weighted[...].astype(jnp.bfloat16).reshape(half, block_rows, LAT)
-        msg[slots, :, LAT:] = stats.astype(jnp.bfloat16).reshape(half, block_rows, LANES)
+        msg[slots] = weighted[...].astype(jnp.bfloat16).reshape(half, block_rows, LAT)
         for k in range(turn, half):
             to = part_side * half + lax.rem(place + k, half)
             slot = turn * half + k
@@ -261,20 +267,32 @@
             )
             copy.start()
             m_copies.append(copy)
+            copy = pltpu.make_async_remote_copy(
+                src_ref=stat_msg.at[turn],
+                dst_ref=stat_got.at[slot],
+                send_sem=s_send.at[slot],
+                recv_sem=s_recv.at[slot],
+                device_id=(to, me_tp),
+                device_id_type=MESH,
+            )
+            copy.start()
+            m_copies.append(copy)
     got[half] = msg[me]
+    stat_got[half] = stat_msg[1]
     uv_load.wait()
     for copy in m_copies:
         copy.wait()
 
-    tops, totals = [], []
     for k in range(n):
-        stat = got[k, :, LAT:].astype(jnp.float32)
-        tops.append(stat[:, 0:1] + stat[:, 1:2] + stat[:, 2:3])
-        totals.append(stat[:, 3:4] + stat[:, 4:5] + stat[:, 5:6])
+        stat_rows[2 * k : 2 * k + 2, :] = stat_got[k]
+    stat_columns[...] = jnp.transpose(stat_rows[...])
+    stat = stat_columns[pl.ds(pl.multiple_of(place * block_rows, block_rows), block_rows), :]
+    tops = [stat[:, 2 * k : 2 * k + 1] for k in range(n)]
+    totals = [stat[:, 2 * k + 1 : 2 * k + 2] for k in range(n)]
     best = functools.reduce(jnp.maximum, tops)
     factors = [jnp.exp2(top - best) for top in tops]
     whole = sum(f * m for f, m in zip(factors, totals))
-    latent = sum(f * got[k, :, :LAT].astype(jnp.float32) for k, f in enumerate(factors)) / whole
+    latent = sum(f * got[k].astype(jnp.float32) for k, f in enumerate(factors)) / whole
     values = []
     for j in range(block_heads):
         pieces = jnp.concatenate(thirds(latent[j * head_rows : (j + 1) * head_rows]), axis=0)
@@ -400,8 +418,12 @@
             pltpu.VMEM((rows // 2, LANES), f32),
             pltpu.VMEM((rows // 2, LANES), f32),
             pltpu.VMEM((rows // 2, LAT), f32),
-            pltpu.VMEM((n, block_rows, LAT + LANES), bf),
-            pltpu.VMEM((n, block_rows, LAT + LANES), bf),
+            pltpu.VMEM((n, block_rows, LAT), bf),
+            pltpu.VMEM((n, block_rows, LAT), bf),
+            pltpu.VMEM((2, 2, rows // 2), f32),
+            pltpu.VMEM((n, 2, rows // 2), f32),
+            pltpu.VMEM((LANES, rows // 2), f32),
+            pltpu.VMEM((rows // 2, LANES), f32),
             pltpu.VMEM((n, head_rows, block_heads * vdim), bf),
             pltpu.VMEM((t, share, columns), f32),
             pltpu.VMEM((t, share, columns), f32),
@@ -411,6 +433,8 @@
             dma((4,)),
             dma((2, n)),
             dma((2, n)),
+            dma((n,)),
+            dma((n,)),
             dma((n,)),
             dma((n,)),
             dma((n,)),

time: 35.3 us -> 34.8 us (0.986)
  Pallas kernels: 33.2 us -> 32.7 us
    pallas_call x1, Pallas kernels: 33.2 us -> 32.7 us  [on_device(): pl.pallas_call(functools.partial(kernel, sizes), out_shape=jax.ShapeDtype...]
where the time goes in v4:
time: 34.8 us; the launch traced here: 34.6 us
  Pallas kernels  32.7 us (94%)
  local copies, waits for them, and re-layouts  1.27 us (4%)
  between operations  0.66 us (2%)
    pallas_call x1, Pallas kernels, on_device(): pl.pallas_call(functools.partial(kernel, sizes), out_shape=jax.ShapeDtype...  32.7 us
    unnamed x1, local copies, waits for them, and re-layouts  1.27 us

profile of v4, /device:TPU:0, one launch (start us, length us, event | category | flops | bytes accessed | tf_op | source)
XLA Modules:
  0.0 34.6 jit_solution(10904389994250588446)
XLA Ops:
  0.7 32.7 %shard_map.100 = bf16[2,896]{1,0:T(2,128)(2,1)} custom-call(s32[1]{0:T(128)S(6)} %copy.12.suffix_len_ref, s32[64]{0:T(128)} %table_hbm.1, s32[8]{0:T(128)} %prefix_len_hbm.1, bf16[1,32,128]{2,1,0:T(8,128)(2,1)} %q_nope_ref.1, bf16[1,32,64]{2,1,0:T(8,128)(2,1)} %q_rope_ref.1, bf16[32,128,512]{2,1,0:T(8,128)(2,1)} %w_uk_hbm.1, bf16[32,512,128]{2,1,0:T(8,128)(2,1)} %w_uv_hbm.1, ...), custom_call_target="tpu_custom_call" | custom-call | tf_op jit(solution)/shard_map/pallas_call | solution.py:402
  33.4 1.3 %copy.13 = bf16[2,896]{1,0:T(2,128)(2,1)} copy(bf16[2,896]{1,0:T(2,128)(2,1)} %shard_map.100) | data formatting | bytes 7168

commit v5 on v4

--- a/solution.py
+++ b/solution.py
@@ -187,7 +187,7 @@
         shuffle, qr_all[...].reshape(rows, ROPE), preferred_element_type=jnp.float32
     ).astype(jnp.bfloat16)
     loads[0].wait()
-    group = 8
+    group = heads
 
     def absorb(g, carry):
         latents = []
@@ -226,34 +226,34 @@
             )
             s = (s * scale).reshape(part_rows // requests, requests, length)
             s = (s + mask[:, start : start + length][None]).reshape(part_rows, length)
-            scores[:, start : start + length] = s
+            scores[turn, :, start : start + length] = s
             top = s[:, :LANES]
             for j in range(1, length // LANES):
                 top = jnp.maximum(top, s[:, j * LANES : (j + 1) * LANES])
-            peak[...] = top if i == 0 else jnp.maximum(peak[...], top)
-        highest = jnp.maximum(jnp.max(peak[...], axis=1, keepdims=True), FLOOR)
-        peak[...] = jnp.broadcast_to(highest, (part_rows, LANES))
+            peak[turn] = top if i == 0 else jnp.maximum(peak[turn], top)
+        highest = jnp.maximum(jnp.max(peak[turn], axis=1, keepdims=True), FLOOR)
+        peak[turn] = jnp.broadcast_to(highest, (part_rows, LANES))
         for i, (start, length) in enumerate(spans):
-            p = jnp.exp2(scores[:, start : start + length] - peak[:, :1]).astype(jnp.bfloat16)
+            p = jnp.exp2(scores[turn, :, start : start + length] - peak[turn, :, :1]).astype(jnp.bfloat16)
             wide = p.astype(jnp.float32)
             total = wide[:, :LANES]
             for j in range(1, length // LANES):
                 total = total + wide[:, j * LANES : (j + 1) * LANES]
-            mass[...] = total if i == 0 else mass[...] + total
+            mass[turn] = total if i == 0 else mass[turn] + total
             term = lax.dot_general(
                 p,
                 cache[:LAT, start : start + length],
                 (((1,), (1,)), ((), ())),
                 preferred_element_type=jnp.float32,
             )
-            weighted[...] = term if i == 0 else weighted[...] + term
-
-        sums = jnp.sum(mass[...], axis=1, keepdims=True)
+            weighted[turn] = term if i == 0 else weighted[turn] + term
+
+        sums = jnp.sum(mass[turn], axis=1, keepdims=True)
         at_lane = lax.broadcasted_iota(jnp.int32, (part_rows, LANES), 1)
-        stats = jnp.where(at_lane == 0, peak[...], sums)
+        stats = jnp.where(at_lane == 0, peak[turn], sums)
         stat_msg[turn] = jnp.transpose(stats)[:2]
         slots = pl.ds(part_side * half, half)
-        msg[slots] = weighted[...].astype(jnp.bfloat16).reshape(half, block_rows, LAT)
+        msg[slots] = weighted[turn].astype(jnp.bfloat16).reshape(half, block_rows, LAT)
         for k in range(turn, half):
             to = part_side * half + lax.rem(place + k, half)
             slot = turn * half + k
@@ -340,9 +340,6 @@
                 lhs, w_out[h * vdim : (h + 1) * vdim, :], preferred_element_type=jnp.float32
             )
             total = term if h == 0 else total + term
-    for copy in h_copies:
-        copy.wait_send()
-
     share = requests // t
     for i in range(t):
         part[i] = total[i * share : (i + 1) * share]
@@ -359,6 +356,8 @@
         )
         copy.start()
         p_copies.append(copy)
+    for copy in h_copies:
+        copy.wait_send()
     result = part[me_tp]
     for k in range(1, t):
         p_copies[k - 1].wait()
@@ -384,7 +383,7 @@
     requests = own * n
     tokens, width = prefix_cache.shape
     suffix = suffix_cache.shape[1]
-    chunk = 2048 if tokens % 2048 == 0 else tokens
+    chunk = 4096 if tokens % 4096 == 0 else tokens
     chunks = tokens // chunk
     slots = tokens + own * suffix
     rows = requests * heads
@@ -414,10 +413,10 @@
             pltpu.VMEM(w_out.shape, bf),
             pltpu.VMEM((width, slots), bf),
             pltpu.VMEM((requests, slots), f32),
-            pltpu.VMEM((rows // 2, slots), f32),
-            pltpu.VMEM((rows // 2, LANES), f32),
-            pltpu.VMEM((rows // 2, LANES), f32),
-            pltpu.VMEM((rows // 2, LAT), f32),
+            pltpu.VMEM((2, rows // 2, slots), f32),
+            pltpu.VMEM((2, rows // 2, LANES), f32),
+            pltpu.VMEM((2, rows // 2, LANES), f32),
+            pltpu.VMEM((2, rows // 2, LAT), f32),
             pltpu.VMEM((n, block_rows, LAT), bf),
             pltpu.VMEM((n, block_rows, LAT), bf),
             pltpu.VMEM((2, 2, rows // 2), f32),

time: 34.8 us -> 34.2 us (0.983)
  Pallas kernels: 32.7 us -> 32.1 us
    pallas_call x1, Pallas kernels: 32.7 us -> 32.1 us  [on_device(): pl.pallas_call(functools.partial(kernel, sizes), out_shape=jax.ShapeDtype...]
where the time goes in v5:
time: 34.2 us; the launch traced here: 34 us
  Pallas kernels  32.1 us (94%)
  local copies, waits for them, and re-layouts  1.27 us (4%)
  between operations  0.66 us (2%)
    pallas_call x1, Pallas kernels, on_device(): pl.pallas_call(functools.partial(kernel, sizes), out_shape=jax.ShapeDtype...  32.1 us
    unnamed x1, local copies, waits for them, and re-layouts  1.27 us

profile of v5, /device:TPU:0, one launch (start us, length us, event | category | flops | bytes accessed | tf_op | source)
XLA Modules:
  0.0 34.0 jit_solution(2605769932737662932)
XLA Ops:
  0.7 32.1 %shard_map.100 = bf16[2,896]{1,0:T(2,128)(2,1)} custom-call(s32[1]{0:T(128)S(6)} %copy.12.suffix_len_ref, s32[64]{0:T(128)} %table_hbm.1, s32[8]{0:T(128)} %prefix_len_hbm.1, bf16[1,32,128]{2,1,0:T(8,128)(2,1)} %q_nope_ref.1, bf16[1,32,64]{2,1,0:T(8,128)(2,1)} %q_rope_ref.1, bf16[32,128,512]{2,1,0:T(8,128)(2,1)} %w_uk_hbm.1, bf16[32,512,128]{2,1,0:T(8,128)(2,1)} %w_uv_hbm.1, ...), custom_call_target="tpu_custom_call" | custom-call | tf_op jit(solution)/shard_map/pallas_call | solution.py:401
  32.8 1.3 %copy.13 = bf16[2,896]{1,0:T(2,128)(2,1)} copy(bf16[2,896]{1,0:T(2,128)(2,1)} %shard_map.100) | data formatting | bytes 7168
